TPU v7x, 256 devices: a whole 4x4x8 slice. The times are simulated.
256 devices in a mesh: phi: 64 (over z, x, y_lo), row: 4 (over y_hi, core).
Axes of the slice: x: 4, y: 4 (y_hi: 2, y_lo: 2; y = y_hi * 2 + y_lo), z: 8, core: 2. Of those that a mesh axis runs over, the one named last changes fastest.
Arguments:
- density: float32 [1024, 32, 512], P('phi', None, 'row'), may hold values from 0.5 to 2
- velocity: float32 [3, 1024, 32, 512], P(None, 'phi', None, 'row'), may hold values from -0.3 to 0.3
- shifts: int32 [64], P('row'), may hold values from 0 to 255, as said below
- fractions: float32 [64], P('row'), may hold values from 0 to 1
Outputs:
- density_out: float32 [1024, 32, 512], P('phi', None, 'row')
- stepped_velocity: float32 [3, 1024, 32, 512], P(None, 'phi', None, 'row')
- image: float32 [1024, 1024], P(('phi', 'row'))
Inputs may be any that keep to these rules, and one draw needn't show every extreme that they name: `shifts`: some band has shift 0 and some band has shift 256 - 1.
All inputs are finite; a program needn't handle non-finite values.
Results may differ from a plain program's by a relative error of at most 0.000071.
Values sent between devices are 32-bit elements; how exact they have to be, the bound alone decides.
A program may use at most 64 MiB of HBM per device.

v0:
```python
import jax
import jax.numpy as jnp
from jax import lax
from jax.sharding import PartitionSpec as P

BAND = 8
STEPS = 2
NPIX = 1024
SPEED = 1.5
COURANT = 0.05
KAPPA = 1.5
R_INNER = 0.2


def padded(cells, sides, width, closed):
    for axis, dim in sides:
        count = lax.axis_size(axis)
        ends = count if closed else count - 1
        head = lax.slice_in_dim(cells, 0, width, axis=dim)
        tail = lax.slice_in_dim(cells, cells.shape[dim] - width, cells.shape[dim], axis=dim)
        cells = jnp.concatenate(
            [
                lax.ppermute(tail, axis, [(i, (i + 1) % count) for i in range(ends)]),
                cells,
                lax.ppermute(head, axis, [((i + 1) % count, i) for i in range(ends)]),
            ],
            axis=dim,
        )
    return cells


def passed_along(value, axis, steps):
    count = lax.axis_size(axis)
    pairs = [(source, (source + steps) % count) for source in range(count)]
    return lax.ppermute(value, axis, pairs)


def conserved(prim):
    rho = prim[0]
    return jnp.stack([rho, rho * prim[1], rho * prim[2], rho * prim[3]])


def divergence(extended, axis, comp):
    cons = conserved(extended)
    flux = cons * extended[comp][None]
    flux = flux.at[comp].add(extended[0])
    size = extended.shape[axis]
    low_c = lax.slice_in_dim(cons, 0, size - 1, axis=axis)
    high_c = lax.slice_in_dim(cons, 1, size, axis=axis)
    low_f = lax.slice_in_dim(flux, 0, size - 1, axis=axis)
    high_f = lax.slice_in_dim(flux, 1, size, axis=axis)
    face = 0.5 * (low_f + high_f) - 0.5 * SPEED * (high_c - low_c)
    return lax.slice_in_dim(face, 1, size - 1, axis=axis) - lax.slice_in_dim(
        face, 0, size - 2, axis=axis
    )


def advance(prim, ext_phi, padded_polar_grid, ext_radial):
    total = (
        divergence(ext_phi, 1, 2)
        + divergence(padded_polar_grid, 2, 3)
        + divergence(ext_radial, 3, 1)
    )
    fresh = conserved(prim) - COURANT * total
    rho = fresh[0]
    return jnp.stack([rho, fresh[1] / rho, fresh[2] / rho, fresh[3] / rho])


def column_light(rho, radial_index, total_radial):
    polar = rho.shape[1]
    dtau = KAPPA / polar * rho
    above = jnp.cumsum(dtau, axis=1) - dtau
    theta = (jnp.arange(polar, dtype=jnp.int32).astype(jnp.float32) + 0.5) / polar
    tilt = 1.0 + 0.5 * jnp.cos(jnp.pi * theta)
    radius = R_INNER + (radial_index.astype(jnp.float32) + 0.5) * (1.0 - R_INNER) / total_radial
    source = (1.0 / jnp.sqrt(radius))[None, None, :] * tilt[None, :, None]
    return jnp.sum(source * (1.0 - jnp.exp(-dtau)) * jnp.exp(-above), axis=1)


def pixel_corners(pixel_rows, npix, nphi, nrad):
    yy = ((pixel_rows.astype(jnp.float32) + 0.5) / npix * 2.0 - 1.0)[:, None]
    xx = ((jnp.arange(npix, dtype=jnp.int32).astype(jnp.float32) + 0.5) / npix * 2.0 - 1.0)[None, :]
    dist = jnp.sqrt(xx * xx + yy * yy)
    upos = (dist - R_INNER) / (1.0 - R_INNER) * nrad - 0.5
    radial_floor_index = jnp.floor(upos)
    radial_fraction = upos - radial_floor_index
    radial_lower_index = radial_floor_index.astype(jnp.int32)
    angle = jnp.arctan2(yy, xx)
    vpos = (angle + jnp.pi) / (2.0 * jnp.pi) * nphi - 0.5
    lfloor = jnp.floor(vpos)
    polar_fraction = vpos - lfloor
    polar_lower_index = lfloor.astype(jnp.int32) % nphi
    polar_upper_index = (polar_lower_index + 1) % nphi
    return [
        (polar_lower_index, radial_lower_index, (1.0 - polar_fraction) * (1.0 - radial_fraction)),
        (polar_upper_index, radial_lower_index, polar_fraction * (1.0 - radial_fraction)),
        (polar_lower_index, radial_lower_index + 1, (1.0 - polar_fraction) * radial_fraction),
        (polar_upper_index, radial_lower_index + 1, polar_fraction * radial_fraction),
    ]


def sample_block(table, corners, l_first, k_first):
    nl, nk = table.shape
    flat = table.reshape(-1)
    total = jnp.zeros(corners[0][2].shape, table.dtype)
    for lidx, kidx, weight in corners:
        lloc = lidx - l_first
        kloc = kidx - k_first
        valid = (lloc >= 0) & (lloc < nl) & (kloc >= 0) & (kloc < nk)
        spot = jnp.clip(lloc, 0, nl - 1) * nk + jnp.clip(kloc, 0, nk - 1)
        total = total + jnp.where(valid, weight * jnp.take(flat, spot), 0.0)
    return total


def body(density, velocity, shifts, fractions):
    cycle = lax.axis_size("phi")
    bands = lax.axis_size("row")
    cells = density.shape[0]
    radial = density.shape[2]
    nphi = cells * cycle
    nrad = radial * bands
    prim = jnp.concatenate([density[None], velocity], axis=0)
    shift_col = jnp.repeat(shifts, BAND)
    frac_col = jnp.repeat(fractions, BAND)
    whole = shift_col // cells
    remain = shift_col % cells
    levels = (cycle // 4 - 1).bit_length()
    for step in range(STEPS):
        ext_phi = padded(prim, (("phi", 1),), 1, True)
        ext_radial = padded(prim, (("row", 3),), 1, False)
        padded_polar_grid = jnp.pad(prim, ((0, 0), (0, 0), (1, 1), (0, 0)))
        prim = advance(prim, ext_phi, padded_polar_grid, ext_radial)
        for level in range(levels):
            moved = passed_along(prim, "phi", 2**level)
            taken = whole // 2**level % 2 == 1
            prim = jnp.where(taken[None, None, None, :], moved, prim)
        left = passed_along(prim, "phi", 1)
        joined = jnp.concatenate([left, prim], axis=1)
        lead = lax.slice_in_dim(joined, cells, 2 * cells, axis=1)
        trail = lax.slice_in_dim(joined, cells - 1, 2 * cells - 1, axis=1)
        for offset in range(1, cells):
            picked = (remain == offset)[None, None, None, :]
            lead = jnp.where(
                picked, lax.slice_in_dim(joined, cells - offset, 2 * cells - offset, axis=1), lead
            )
            trail = jnp.where(
                picked,
                lax.slice_in_dim(joined, cells - offset - 1, 2 * cells - offset - 1, axis=1),
                trail,
            )
        prim = (1.0 - frac_col) * lead + frac_col * trail
    radial_index = lax.axis_index("row") * radial + jnp.arange(radial, dtype=jnp.int32)
    intensity = column_light(prim[0], radial_index, nrad)
    rows_dev = NPIX // (cycle * bands)
    first_row = (lax.axis_index("phi") * bands + lax.axis_index("row")) * rows_dev
    pixel_rows = first_row + jnp.arange(rows_dev, dtype=jnp.int32)
    table = lax.all_gather(intensity, "row", axis=1, tiled=True)
    table = lax.all_gather(table, "phi", axis=0, tiled=True)
    image = sample_block(table, pixel_corners(pixel_rows, NPIX, nphi, nrad), 0, 0)
    return (prim[0], prim[1:], image)


def solution(mesh):
    in_specs = (P("phi", None, "row"), P(None, "phi", None, "row"), P("row"), P("row"))
    out_specs = (P("phi", None, "row"), P(None, "phi", None, "row"), P(("phi", "row"), None))
    return jax.shard_map(body, mesh=mesh, in_specs=in_specs, out_specs=out_specs, check_vma=False)
```

profile of v0, /device:TPU:16, one launch (start us, length us, event | category | flops | bytes accessed | tf_op | source)
XLA Modules:
  0.0 745.6 jit_solution(6598859238169226459)
XLA Ops:
  7.2 1.6 copy.28
  10.7 1.9 collective-permute-start.3
  13.7 2.4 collective-permute-start.2
  16.9 8.9 %collective-permute-start.1 = (f32[4,1,32,128]{3,1,2,0:T(1,128)}, f32[4,1,32,128]{3,1,2,0:T(1,128)S(1)}, u32[]{:S(2)}, u32[]{:S(2)}) collective-permute-start(f32[4,1,32,128]{3,1,2,0:T(1,128)} %get-tuple-element.146), channel_id=1, source_target_pairs={{4,0},{8,4},{12,8},{16,12},{20,16},{24,20},{28,24},{32,28},{36,32}... | collective-permute-start | bytes 196616 | tf_op jit(solution)/shard_map/ppermute | solution.py:25
  27.0 2.2 copy.37
  29.2 2.1 pad_maximum_fusion.2
  38.7 26.5 %collective-permute-done.4 = f32[4,16,32,128]{3,1,2,0:T(8,128)S(1)} collective-permute-done((f32[4,16,32,128]{3,1,2,0:T(8,128)S(1)}, f32[4,16,32,128]{3,1,2,0:T(8,128)S(1)}, u32[]{:S(2)}, u32[]{:S(2)}) %collective-permute-start.4) | collective-permute-done | bytes 1048608 | tf_op jit(solution)/shard_map/ppermute | solution.py:35
  65.4 26.2 %collective-permute-done.5 = f32[4,16,32,128]{3,1,2,0:T(8,128)S(1)} collective-permute-done((f32[4,16,32,128]{3,1,2,0:T(8,128)S(1)}, f32[4,16,32,128]{3,1,2,0:T(8,128)S(1)}, u32[]{:S(2)}, u32[]{:S(2)}) %collective-permute-start.5) | collective-permute-done | bytes 1048608 | tf_op jit(solution)/shard_map/ppermute | solution.py:35
  92.1 27.6 %collective-permute-done.6 = f32[4,16,32,128]{3,1,2,0:T(8,128)S(1)} collective-permute-done((f32[4,16,32,128]{3,1,2,0:T(8,128)S(1)}, f32[4,16,32,128]{3,1,2,0:T(8,128)S(1)}, u32[]{:S(2)}, u32[]{:S(2)}) %collective-permute-start.6) | collective-permute-done | bytes 1048608 | tf_op jit(solution)/shard_map/ppermute | solution.py:35
  119.9 17.4 %collective-permute-done.7 = f32[4,16,32,128]{3,1,2,0:T(8,128)S(1)} collective-permute-done((f32[4,16,32,128]{3,1,2,0:T(8,128)S(1)}, f32[4,16,32,128]{3,1,2,0:T(8,128)S(1)}, u32[]{:S(2)}, u32[]{:S(2)}) %collective-permute-start.7) | collective-permute-done | bytes 1048608 | tf_op jit(solution)/shard_map/ppermute | solution.py:35
  138.6 18.4 %collective-permute-done.8 = f32[4,16,32,128]{3,1,2,0:T(8,128)S(1)} collective-permute-done((f32[4,16,32,128]{3,1,2,0:T(8,128)S(1)}, f32[4,16,32,128]{3,1,2,0:T(8,128)S(1)}, u32[]{:S(2)}, u32[]{:S(2)}) %collective-permute-start.8) | collective-permute-done | bytes 1048608 | tf_op jit(solution)/shard_map/ppermute | solution.py:35
  157.2 3.5 multiply_add_fusion.1
  163.4 17.8 %collective-permute-start.12 = (f32[4,16,32,1]{2,1,3,0:T(8,128)S(1)}, f32[4,16,32,1]{2,1,3,0:T(8,128)}, u32[]{:S(2)}, u32[]{:S(2)}) collective-permute-start(f32[4,16,32,1]{2,1,3,0:T(8,128)S(1)} %copy.40), channel_id=1, source_target_pairs={{1,0},{2,1},{3,2},{5,4},{6,5},{7,6},{9,8},{10,9},{11,10},{13,12},{... | collective-permute-start | bytes 24584 | tf_op jit(solution)/shard_map/ppermute | solution.py:25
  182.3 1.9 collective-permute-start.11
  184.2 1.4 broadcast_multiply_fusion.4
  187.0 1.9 collective-permute-start.9
  188.9 1.3 copy.42
  190.7 2.2 copy.41
  192.9 2.1 pad_maximum_fusion.4
  200.7 28.2 %collective-permute-done.13 = f32[4,16,32,128]{3,1,2,0:T(8,128)S(1)} collective-permute-done((f32[4,16,32,128]{3,1,2,0:T(8,128)S(1)}, f32[4,16,32,128]{3,1,2,0:T(8,128)S(1)}, u32[]{:S(2)}, u32[]{:S(2)}) %collective-permute-start.13) | collective-permute-done | bytes 1048608 | tf_op jit(solution)/shard_map/ppermute | solution.py:35
  229.2 28.3 %collective-permute-done.14 = f32[4,16,32,128]{3,1,2,0:T(8,128)S(1)} collective-permute-done((f32[4,16,32,128]{3,1,2,0:T(8,128)S(1)}, f32[4,16,32,128]{3,1,2,0:T(8,128)S(1)}, u32[]{:S(2)}, u32[]{:S(2)}) %collective-permute-start.14) | collective-permute-done | bytes 1048608 | tf_op jit(solution)/shard_map/ppermute | solution.py:35
  257.7 26.4 %collective-permute-done.15 = f32[4,16,32,128]{3,1,2,0:T(8,128)S(1)} collective-permute-done((f32[4,16,32,128]{3,1,2,0:T(8,128)S(1)}, f32[4,16,32,128]{3,1,2,0:T(8,128)S(1)}, u32[]{:S(2)}, u32[]{:S(2)}) %collective-permute-start.15) | collective-permute-done | bytes 1048608 | tf_op jit(solution)/shard_map/ppermute | solution.py:35
  284.5 16.0 %collective-permute-done.16 = f32[4,16,32,128]{3,1,2,0:T(8,128)S(1)} collective-permute-done((f32[4,16,32,128]{3,1,2,0:T(8,128)S(1)}, f32[4,16,32,128]{3,1,2,0:T(8,128)S(1)}, u32[]{:S(2)}, u32[]{:S(2)}) %collective-permute-start.16) | collective-permute-done | bytes 1048608 | tf_op jit(solution)/shard_map/ppermute | solution.py:35
  300.9 18.9 %collective-permute-done.17 = f32[4,16,32,128]{3,1,2,0:T(8,128)S(1)} collective-permute-done((f32[4,16,32,128]{3,1,2,0:T(8,128)S(1)}, f32[4,16,32,128]{3,1,2,0:T(8,128)S(1)}, u32[]{:S(2)}, u32[]{:S(2)}) %collective-permute-start.17) | collective-permute-done | bytes 1048608 | tf_op jit(solution)/shard_map/ppermute | solution.py:35
  319.9 3.5 multiply_add_fusion
  323.6 19.1 %all_gather.6 = f32[16,512]{1,0:T(8,128)} all-gather(f32[16,128]{1,0:T(8,128)S(1)} %fusion.116), channel_id=1, replica_groups=mesh['phi'=64,'row'=4] {'row'}, dimensions={1}, use_global_device_ids=true | all-gather | bytes 40960 | tf_op jit(solution)/shard_map/all_gather | solution.py:157
  345.0 298.5 %all-gather.2.cloned.1.call-done = f32[1024,512]{1,0:T(8,128)} async-done(((f32[16,512]{1,0:T(8,128)}), f32[1024,512]{1,0:T(8,128)}) %all-gather.2.cloned.1.call-update) | async-done | bytes 2097168 | tf_op jit(solution)/shard_map/all_gather | solution.py:158
  643.5 2.1 copy.45
  645.7 23.0 %gather_fusion.3 = f32[4096]{0:T(1024)S(1)} fusion(f32[524288]{0:T(1024)S(1)} %bitcast.63, s32[4096]{0:T(1024)S(1)} %bitcast_clamp_fusion), kind=kCustom, calls=%fused_computation.3.clone | custom fusion | bytes 49152 | tf_op jit(solution)/shard_map/jit(_take)/gather | solution.py:111
  668.7 23.0 %gather_fusion.2 = f32[4096]{0:T(1024)S(1)} fusion(f32[524288]{0:T(1024)S(1)} %bitcast.64, s32[4096]{0:T(1024)S(1)} %bitcast_clamp_fusion.1), kind=kCustom, calls=%fused_computation.2.clone | custom fusion | bytes 49152 | tf_op jit(solution)/shard_map/jit(_take)/gather | solution.py:111
  691.8 23.0 %gather_fusion.1 = f32[4096]{0:T(1024)S(1)} fusion(f32[524288]{0:T(1024)S(1)} %bitcast.65, s32[4096]{0:T(1024)S(1)} %bitcast_clamp_fusion.2), kind=kCustom, calls=%fused_computation.1.clone | custom fusion | bytes 49152 | tf_op jit(solution)/shard_map/jit(_take)/gather | solution.py:111
  714.8 23.0 %gather_fusion = f32[4096]{0:T(1024)S(1)} fusion(f32[524288]{0:T(1024)S(1)} %bitcast.66, s32[4096]{0:T(1024)S(1)} %bitcast_clamp_fusion.3), kind=kCustom, calls=%fused_computation.clone | custom fusion | bytes 49152 | tf_op jit(solution)/shard_map/jit(_take)/gather | solution.py:111
  (185 shorter events, 29.9 us)
Async XLA Ops:
  7.2 636.4 %all-gather.2.cloned.1.call-start = ((), (), s32[]{:S(2)}) async-start(), calls=%async_computation | async-start | bytes 2129920 | tf_op jit(solution)/shard_map/all_gather | solution.py:158
  10.7 15.8 %collective-permute-start.3 = (f32[4,16,32,1]{2,1,3,0:T(8,128)S(1)}, f32[4,16,32,1]{2,1,3,0:T(8,128)S(1)}, u32[]{:S(2)}, u32[]{:S(2)}) collective-permute-start(f32[4,16,32,1]{2,1,3,0:T(8,128)S(1)} %copy.36), channel_id=1, source_target_pairs={{1,0},{2,1},{3,2},{5,4},{6,5},{7,6},{9,8},{10,9},{11,10},{13,12},{... | collective-permute-start | bytes 24584 | tf_op jit(solution)/shard_map/ppermute | solution.py:25
  13.7 13.3 %collective-permute-start.2 = (f32[4,16,32,1]{2,1,3,0:T(8,128)}, f32[4,16,32,1]{2,1,3,0:T(8,128)}, u32[]{:S(2)}, u32[]{:S(2)}) collective-permute-start(f32[4,16,32,1]{2,1,3,0:T(8,128)} %copy.35), channel_id=1, source_target_pairs={{0,1},{1,2},{2,3},{4,5},{5,6},{6,7},{8,9},{9,10},{10,11},{12,13},{... | collective-permute-start | bytes 24584 | tf_op jit(solution)/shard_map/ppermute | solution.py:23
  16.9 16.7 %collective-permute-start.1 = (f32[4,1,32,128]{3,1,2,0:T(1,128)}, f32[4,1,32,128]{3,1,2,0:T(1,128)S(1)}, u32[]{:S(2)}, u32[]{:S(2)}) collective-permute-start(f32[4,1,32,128]{3,1,2,0:T(1,128)} %get-tuple-element.146), channel_id=1, source_target_pairs={{4,0},{8,4},{12,8},{16,12},{20,16},{24,20},{28,24},{32,28},{36,32}... | collective-permute-start | bytes 196616 | tf_op jit(solution)/shard_map/ppermute | solution.py:25
  25.8 8.8 %collective-permute-start = (f32[4,1,32,128]{3,1,2,0:T(1,128)}, f32[4,1,32,128]{3,1,2,0:T(1,128)}, u32[]{:S(2)}, u32[]{:S(2)}) collective-permute-start(f32[4,1,32,128]{3,1,2,0:T(1,128)} %get-tuple-element.145), channel_id=1, source_target_pairs={{0,4},{4,8},{8,12},{12,16},{16,20},{20,24},{24,28},{28,32},{32,36}... | collective-permute-start | bytes 196616 | tf_op jit(solution)/shard_map/ppermute | solution.py:23
  37.9 27.3 %collective-permute-start.4 = (f32[4,16,32,128]{3,1,2,0:T(8,128)S(1)}, f32[4,16,32,128]{3,1,2,0:T(8,128)S(1)}, u32[]{:S(2)}, u32[]{:S(2)}) collective-permute-start(f32[4,16,32,128]{3,1,2,0:T(8,128)S(1)} %pad_maximum_fusion.14), channel_id=1, source_target_pairs={{0,4},{4,8},{8,12},{12,16},{16,20},{20,24},{24,28},{28,32},{32,36}... | collective-permute-start | bytes 3145736 | tf_op jit(solution)/shard_map/ppermute | solution.py:35
  38.7 81.0 %copy-start.8 = (pred[128]{0:T(512)(128)(4,1)}, pred[128]{0:T(512)(128)(4,1)S(1)}, u32[]{:S(2)}) copy-start(pred[128]{0:T(512)(128)(4,1)S(1)} %get-tuple-element.175) | copy-start | bytes 388
  65.3 26.3 %collective-permute-start.5 = (f32[4,16,32,128]{3,1,2,0:T(8,128)S(1)}, f32[4,16,32,128]{3,1,2,0:T(8,128)S(1)}, u32[]{:S(2)}, u32[]{:S(2)}) collective-permute-start(f32[4,16,32,128]{3,1,2,0:T(8,128)S(1)} %broadcast_select_fusion.1), channel_id=1, source_target_pairs={{0,8},{4,12},{8,16},{12,20},{16,24},{20,28},{24,32},{28,36},{32,40... | collective-permute-start | bytes 3145736 | tf_op jit(solution)/shard_map/ppermute | solution.py:35
  91.8 27.9 %collective-permute-start.6 = (f32[4,16,32,128]{3,1,2,0:T(8,128)S(1)}, f32[4,16,32,128]{3,1,2,0:T(8,128)S(1)}, u32[]{:S(2)}, u32[]{:S(2)}) collective-permute-start(f32[4,16,32,128]{3,1,2,0:T(8,128)S(1)} %broadcast_select_fusion.3), channel_id=1, source_target_pairs={{0,16},{4,20},{8,24},{12,28},{16,32},{20,36},{24,40},{28,44},{32,4... | collective-permute-start | bytes 3145736 | tf_op jit(solution)/shard_map/ppermute | solution.py:35
  119.8 17.5 %collective-permute-start.7 = (f32[4,16,32,128]{3,1,2,0:T(8,128)S(1)}, f32[4,16,32,128]{3,1,2,0:T(8,128)S(1)}, u32[]{:S(2)}, u32[]{:S(2)}) collective-permute-start(f32[4,16,32,128]{3,1,2,0:T(8,128)S(1)} %broadcast_select_fusion.5), channel_id=1, source_target_pairs={{0,32},{4,36},{8,40},{12,44},{16,48},{20,52},{24,56},{28,60},{32,6... | collective-permute-start | bytes 3145736 | tf_op jit(solution)/shard_map/ppermute | solution.py:35
  137.4 19.6 %collective-permute-start.8 = (f32[4,16,32,128]{3,1,2,0:T(8,128)S(1)}, f32[4,16,32,128]{3,1,2,0:T(8,128)S(1)}, u32[]{:S(2)}, u32[]{:S(2)}) collective-permute-start(f32[4,16,32,128]{3,1,2,0:T(8,128)S(1)} %broadcast_select_fusion.7), channel_id=1, source_target_pairs={{0,4},{4,8},{8,12},{12,16},{16,20},{20,24},{24,28},{28,32},{32,36}... | collective-permute-start | bytes 3145736 | tf_op jit(solution)/shard_map/ppermute | solution.py:35
  163.4 25.5 %collective-permute-start.12 = (f32[4,16,32,1]{2,1,3,0:T(8,128)S(1)}, f32[4,16,32,1]{2,1,3,0:T(8,128)}, u32[]{:S(2)}, u32[]{:S(2)}) collective-permute-start(f32[4,16,32,1]{2,1,3,0:T(8,128)S(1)} %copy.40), channel_id=1, source_target_pairs={{1,0},{2,1},{3,2},{5,4},{6,5},{7,6},{9,8},{10,9},{11,10},{13,12},{... | collective-permute-start | bytes 24584 | tf_op jit(solution)/shard_map/ppermute | solution.py:25
  182.3 8.4 %collective-permute-start.11 = (f32[4,16,32,1]{2,1,3,0:T(8,128)}, f32[4,16,32,1]{2,1,3,0:T(8,128)}, u32[]{:S(2)}, u32[]{:S(2)}) collective-permute-start(f32[4,16,32,1]{2,1,3,0:T(8,128)} %copy.39), channel_id=1, source_target_pairs={{0,1},{1,2},{2,3},{4,5},{5,6},{6,7},{8,9},{9,10},{10,11},{12,13},{... | collective-permute-start | bytes 24584 | tf_op jit(solution)/shard_map/ppermute | solution.py:23
  185.7 11.6 %collective-permute-start.10 = (f32[4,1,32,128]{3,1,2,0:T(1,128)}, f32[4,1,32,128]{3,1,2,0:T(1,128)S(1)}, u32[]{:S(2)}, u32[]{:S(2)}) collective-permute-start(f32[4,1,32,128]{3,1,2,0:T(1,128)} %get-tuple-element.130), channel_id=1, source_target_pairs={{4,0},{8,4},{12,8},{16,12},{20,16},{24,20},{28,24},{32,28},{36,32}... | collective-permute-start | bytes 196616 | tf_op jit(solution)/shard_map/ppermute | solution.py:25
  187.0 10.2 %collective-permute-start.9 = (f32[4,1,32,128]{3,1,2,0:T(1,128)}, f32[4,1,32,128]{3,1,2,0:T(1,128)}, u32[]{:S(2)}, u32[]{:S(2)}) collective-permute-start(f32[4,1,32,128]{3,1,2,0:T(1,128)} %get-tuple-element.129), channel_id=1, source_target_pairs={{0,4},{4,8},{8,12},{12,16},{16,20},{20,24},{24,28},{28,32},{32,36}... | collective-permute-start | bytes 196616 | tf_op jit(solution)/shard_map/ppermute | solution.py:23
  200.7 28.3 %collective-permute-start.13 = (f32[4,16,32,128]{3,1,2,0:T(8,128)S(1)}, f32[4,16,32,128]{3,1,2,0:T(8,128)S(1)}, u32[]{:S(2)}, u32[]{:S(2)}) collective-permute-start(f32[4,16,32,128]{3,1,2,0:T(8,128)S(1)} %pad_maximum_fusion.15), channel_id=1, source_target_pairs={{0,4},{4,8},{8,12},{12,16},{16,20},{20,24},{24,28},{28,32},{32,36}... | collective-permute-start | bytes 3145736 | tf_op jit(solution)/shard_map/ppermute | solution.py:35
  229.1 55.0 %copy-start.9 = (pred[128]{0:T(512)(128)(4,1)S(1)}, pred[128]{0:T(512)(128)(4,1)}, u32[]{:S(2)}) copy-start(pred[128]{0:T(512)(128)(4,1)} %copy-done.8) | copy-start | bytes 388
  229.1 28.4 %collective-permute-start.14 = (f32[4,16,32,128]{3,1,2,0:T(8,128)S(1)}, f32[4,16,32,128]{3,1,2,0:T(8,128)S(1)}, u32[]{:S(2)}, u32[]{:S(2)}) collective-permute-start(f32[4,16,32,128]{3,1,2,0:T(8,128)S(1)} %broadcast_select_fusion), channel_id=1, source_target_pairs={{0,8},{4,12},{8,16},{12,20},{16,24},{20,28},{24,32},{28,36},{32,40... | collective-permute-start | bytes 3145736 | tf_op jit(solution)/shard_map/ppermute | solution.py:35
  257.7 26.5 %collective-permute-start.15 = (f32[4,16,32,128]{3,1,2,0:T(8,128)S(1)}, f32[4,16,32,128]{3,1,2,0:T(8,128)S(1)}, u32[]{:S(2)}, u32[]{:S(2)}) collective-permute-start(f32[4,16,32,128]{3,1,2,0:T(8,128)S(1)} %broadcast_select_fusion.2), channel_id=1, source_target_pairs={{0,16},{4,20},{8,24},{12,28},{16,32},{20,36},{24,40},{28,44},{32,4... | collective-permute-start | bytes 3145736 | tf_op jit(solution)/shard_map/ppermute | solution.py:35
  284.3 35.5 %copy-start.7 = (f32[128]{0:T(128)S(1)}, f32[128]{0:T(128)}, u32[]{:S(2)}) copy-start(f32[128]{0:T(128)} %copy-done.6) | copy-start | bytes 1540
  284.3 35.5 %copy-start.11 = (pred[128]{0:T(512)(128)(4,1)S(1)}, pred[128]{0:T(512)(128)(4,1)}, u32[]{:S(2)}) copy-start(pred[128]{0:T(512)(128)(4,1)} %copy-done.10) | copy-start | bytes 388
  284.3 35.5 %copy-start.13 = (pred[128]{0:T(512)(128)(4,1)S(1)}, pred[128]{0:T(512)(128)(4,1)}, u32[]{:S(2)}) copy-start(pred[128]{0:T(512)(128)(4,1)} %copy-done.12) | copy-start | bytes 388
  284.3 35.5 %copy-start.15 = (pred[128]{0:T(512)(128)(4,1)S(1)}, pred[128]{0:T(512)(128)(4,1)}, u32[]{:S(2)}) copy-start(pred[128]{0:T(512)(128)(4,1)} %copy-done.14) | copy-start | bytes 388
  284.3 35.5 %copy-start.17 = (pred[128]{0:T(512)(128)(4,1)S(1)}, pred[128]{0:T(512)(128)(4,1)}, u32[]{:S(2)}) copy-start(pred[128]{0:T(512)(128)(4,1)} %copy-done.16) | copy-start | bytes 388
  284.3 35.5 %copy-start.19 = (pred[128]{0:T(512)(128)(4,1)S(1)}, pred[128]{0:T(512)(128)(4,1)}, u32[]{:S(2)}) copy-start(pred[128]{0:T(512)(128)(4,1)} %copy-done.18) | copy-start | bytes 388
  284.3 35.5 %copy-start.21 = (pred[128]{0:T(512)(128)(4,1)S(1)}, pred[128]{0:T(512)(128)(4,1)}, u32[]{:S(2)}) copy-start(pred[128]{0:T(512)(128)(4,1)} %copy-done.20) | copy-start | bytes 388
  284.3 35.5 %copy-start.23 = (pred[128]{0:T(512)(128)(4,1)S(1)}, pred[128]{0:T(512)(128)(4,1)}, u32[]{:S(2)}) copy-start(pred[128]{0:T(512)(128)(4,1)} %copy-done.22) | copy-start | bytes 388
  284.3 35.5 %copy-start.25 = (pred[128]{0:T(512)(128)(4,1)S(1)}, pred[128]{0:T(512)(128)(4,1)}, u32[]{:S(2)}) copy-start(pred[128]{0:T(512)(128)(4,1)} %copy-done.24) | copy-start | bytes 388
  284.4 35.5 %copy-start.27 = (pred[128]{0:T(512)(128)(4,1)S(1)}, pred[128]{0:T(512)(128)(4,1)}, u32[]{:S(2)}) copy-start(pred[128]{0:T(512)(128)(4,1)} %copy-done.26) | copy-start | bytes 388
  284.4 35.5 %copy-start.29 = (pred[128]{0:T(512)(128)(4,1)S(1)}, pred[128]{0:T(512)(128)(4,1)}, u32[]{:S(2)}) copy-start(pred[128]{0:T(512)(128)(4,1)} %copy-done.28) | copy-start | bytes 388
  284.4 16.1 %collective-permute-start.16 = (f32[4,16,32,128]{3,1,2,0:T(8,128)S(1)}, f32[4,16,32,128]{3,1,2,0:T(8,128)S(1)}, u32[]{:S(2)}, u32[]{:S(2)}) collective-permute-start(f32[4,16,32,128]{3,1,2,0:T(8,128)S(1)} %broadcast_select_fusion.4), channel_id=1, source_target_pairs={{0,32},{4,36},{8,40},{12,44},{16,48},{20,52},{24,56},{28,60},{32,6... | collective-permute-start | bytes 3145736 | tf_op jit(solution)/shard_map/ppermute | solution.py:35
  300.7 19.1 %collective-permute-start.17 = (f32[4,16,32,128]{3,1,2,0:T(8,128)S(1)}, f32[4,16,32,128]{3,1,2,0:T(8,128)S(1)}, u32[]{:S(2)}, u32[]{:S(2)}) collective-permute-start(f32[4,16,32,128]{3,1,2,0:T(8,128)S(1)} %broadcast_select_fusion.6), channel_id=1, source_target_pairs={{0,4},{4,8},{8,12},{12,16},{16,20},{20,24},{24,28},{28,32},{32,36}... | collective-permute-start | bytes 3145736 | tf_op jit(solution)/shard_map/ppermute | solution.py:35
  (29 other events, 483.1 us)
Sparse Core Ops, SparseCore 0:
  342.9 300.6 all-gather.1
where the time goes:
time: 746 us
  waiting for transfers between devices  534 us (72%)
  local copies, waits for them, and re-layouts  111 us (15%)
  starting transfers between devices  36.9 us (5%)
  other arithmetic  30 us (4%)
  blocking collectives  19.1 us (3%)
  between operations  15.2 us (2%)
    all_gather x1, waiting for transfers between devices, body(): table = lax.all_gather(table, 'phi', axis=0, tiled=True)  299 us
    ppermute x10, waiting for transfers between devices, passed_along(): return lax.ppermute(value, axis, pairs)  234 us
    gather x8, local copies, waits for them, and re-layouts, sample_block(): total = total + jnp.where(valid, weight * jnp.take(flat, spot), 0.0)  92.2 us
    ppermute x4, starting transfers between devices, padded(): lax.ppermute(head, axis, [((i + 1) % count, i) for i in range(ends)])  28.9 us
    all_gather x1, blocking collectives, body(): table = lax.all_gather(intensity, 'row', axis=1, tiled=True)  19.1 us
  transfers between devices with their start and end apart: 19, of which 13 were waited for; matrix products, arithmetic and copies ran while one was open for 3% of the time, Pallas kernels for 0%

commit v1 on v0

--- a/solution.py
+++ b/solution.py
@@ -155,7 +155,9 @@
     first_row = (lax.axis_index("phi") * bands + lax.axis_index("row")) * rows_dev
     pixel_rows = first_row + jnp.arange(rows_dev, dtype=jnp.int32)
     table = lax.all_gather(intensity, "row", axis=1, tiled=True)
-    table = lax.all_gather(table, "phi", axis=0, tiled=True)
+    table = jnp.concatenate(
+        lax.all_to_all(jnp.stack([table] * lax.axis_size("phi")), "phi", 0, 0), axis=0
+    )
     image = sample_block(table, pixel_corners(pixel_rows, NPIX, nphi, nrad), 0, 0)
     return (prim[0], prim[1:], image)
 

time: 746 us -> 503 us (0.67)
  the two profiles are of different devices: /device:TPU:16 before, /device:TPU:2 now
where the time goes in v1:
time: 503 us; the launch traced here: 493 us
  waiting for transfers between devices  302 us (60%)
  local copies, waits for them, and re-layouts  113 us (22%)
  starting transfers between devices  39.3 us (8%)
  other arithmetic  30 us (6%)
  blocking collectives  6.9 us (1%)
    ppermute x10, waiting for transfers between devices, passed_along(): return lax.ppermute(value, axis, pairs)  252 us
    gather x8, local copies, waits for them, and re-layouts, sample_block(): total = total + jnp.where(valid, weight * jnp.take(flat, spot), 0.0)  92.2 us
    all_to_all x1, waiting for transfers between devices, body(): lax.all_to_all(jnp.stack([table] * lax.axis_size('phi')), 'phi', 0, 0)  49 us
    ppermute x10, starting transfers between devices, passed_along(): return lax.ppermute(value, axis, pairs)  14.8 us
  transfers between devices with their start and end apart: 19, of which 12 were waited for; matrix products, arithmetic and copies ran while one was open for 5% of the time, Pallas kernels for 0%

profile of v1, /device:TPU:2, one launch (start us, length us, event | category | flops | bytes accessed | tf_op | source)
XLA Modules:
  0.0 493.5 jit_solution(3652348346096347184)
XLA Ops:
  0.6 1.6 copy.28
  6.5 3.6 collective-permute-start.2
  10.9 1.5 collective-permute-start.1
  14.1 2.2 copy.37
  16.3 2.1 pad_maximum_fusion.2
  24.0 2.6 collective-permute-start.4
  26.8 25.0 %collective-permute-done.4 = f32[4,16,32,128]{3,1,2,0:T(8,128)S(1)} collective-permute-done((f32[4,16,32,128]{3,1,2,0:T(8,128)S(1)}, f32[4,16,32,128]{3,1,2,0:T(8,128)S(1)}, u32[]{:S(2)}, u32[]{:S(2)}) %collective-permute-start.4) | collective-permute-done | bytes 1048608 | tf_op jit(solution)/shard_map/ppermute | solution.py:35
  52.0 34.0 %collective-permute-done.5 = f32[4,16,32,128]{3,1,2,0:T(8,128)S(1)} collective-permute-done((f32[4,16,32,128]{3,1,2,0:T(8,128)S(1)}, f32[4,16,32,128]{3,1,2,0:T(8,128)S(1)}, u32[]{:S(2)}, u32[]{:S(2)}) %collective-permute-start.5) | collective-permute-done | bytes 1048608 | tf_op jit(solution)/shard_map/ppermute | solution.py:35
  86.8 27.9 %collective-permute-done.6 = f32[4,16,32,128]{3,1,2,0:T(8,128)S(1)} collective-permute-done((f32[4,16,32,128]{3,1,2,0:T(8,128)S(1)}, f32[4,16,32,128]{3,1,2,0:T(8,128)S(1)}, u32[]{:S(2)}, u32[]{:S(2)}) %collective-permute-start.6) | collective-permute-done | bytes 1048608 | tf_op jit(solution)/shard_map/ppermute | solution.py:35
  114.9 24.7 %collective-permute-done.7 = f32[4,16,32,128]{3,1,2,0:T(8,128)S(1)} collective-permute-done((f32[4,16,32,128]{3,1,2,0:T(8,128)S(1)}, f32[4,16,32,128]{3,1,2,0:T(8,128)S(1)}, u32[]{:S(2)}, u32[]{:S(2)}) %collective-permute-start.7) | collective-permute-done | bytes 1048608 | tf_op jit(solution)/shard_map/ppermute | solution.py:35
  140.6 22.7 %collective-permute-done.8 = f32[4,16,32,128]{3,1,2,0:T(8,128)S(1)} collective-permute-done((f32[4,16,32,128]{3,1,2,0:T(8,128)S(1)}, f32[4,16,32,128]{3,1,2,0:T(8,128)S(1)}, u32[]{:S(2)}, u32[]{:S(2)}) %collective-permute-start.8) | collective-permute-done | bytes 1048608 | tf_op jit(solution)/shard_map/ppermute | solution.py:35
  163.3 3.5 multiply_add_fusion.1
  172.0 3.6 collective-permute-start.11
  177.2 3.1 collective-permute-start.10
  182.8 2.2 copy.41
  185.0 2.1 pad_maximum_fusion.4
  193.5 27.8 %collective-permute-done.13 = f32[4,16,32,128]{3,1,2,0:T(8,128)S(1)} collective-permute-done((f32[4,16,32,128]{3,1,2,0:T(8,128)S(1)}, f32[4,16,32,128]{3,1,2,0:T(8,128)S(1)}, u32[]{:S(2)}, u32[]{:S(2)}) %collective-permute-start.13) | collective-permute-done | bytes 1048608 | tf_op jit(solution)/shard_map/ppermute | solution.py:35
  221.5 27.5 %collective-permute-done.14 = f32[4,16,32,128]{3,1,2,0:T(8,128)S(1)} collective-permute-done((f32[4,16,32,128]{3,1,2,0:T(8,128)S(1)}, f32[4,16,32,128]{3,1,2,0:T(8,128)S(1)}, u32[]{:S(2)}, u32[]{:S(2)}) %collective-permute-start.14) | collective-permute-done | bytes 1048608 | tf_op jit(solution)/shard_map/ppermute | solution.py:35
  249.4 27.4 %collective-permute-done.15 = f32[4,16,32,128]{3,1,2,0:T(8,128)S(1)} collective-permute-done((f32[4,16,32,128]{3,1,2,0:T(8,128)S(1)}, f32[4,16,32,128]{3,1,2,0:T(8,128)S(1)}, u32[]{:S(2)}, u32[]{:S(2)}) %collective-permute-start.15) | collective-permute-done | bytes 1048608 | tf_op jit(solution)/shard_map/ppermute | solution.py:35
  277.2 21.4 %collective-permute-done.16 = f32[4,16,32,128]{3,1,2,0:T(8,128)S(1)} collective-permute-done((f32[4,16,32,128]{3,1,2,0:T(8,128)S(1)}, f32[4,16,32,128]{3,1,2,0:T(8,128)S(1)}, u32[]{:S(2)}, u32[]{:S(2)}) %collective-permute-start.16) | collective-permute-done | bytes 1048608 | tf_op jit(solution)/shard_map/ppermute | solution.py:35
  298.8 11.0 %collective-permute-start.17 = (f32[4,16,32,128]{3,1,2,0:T(8,128)S(1)}, f32[4,16,32,128]{3,1,2,0:T(8,128)S(1)}, u32[]{:S(2)}, u32[]{:S(2)}) collective-permute-start(f32[4,16,32,128]{3,1,2,0:T(8,128)S(1)} %broadcast_select_fusion.6), channel_id=1, source_target_pairs={{0,4},{4,8},{8,12},{12,16},{16,20},{20,24},{24,28},{28,32},{32,36}... | collective-permute-start | bytes 3145736 | tf_op jit(solution)/shard_map/ppermute | solution.py:35
  310.0 13.7 %collective-permute-done.17 = f32[4,16,32,128]{3,1,2,0:T(8,128)S(1)} collective-permute-done((f32[4,16,32,128]{3,1,2,0:T(8,128)S(1)}, f32[4,16,32,128]{3,1,2,0:T(8,128)S(1)}, u32[]{:S(2)}, u32[]{:S(2)}) %collective-permute-start.17) | collective-permute-done | bytes 1048608 | tf_op jit(solution)/shard_map/ppermute | solution.py:35
  323.8 3.5 multiply_add_fusion
  327.5 6.9 %all_gather.3 = f32[16,512]{1,0:T(8,128)S(1)} all-gather(f32[16,128]{1,0:T(8,128)S(1)} %fusion.116), channel_id=1, replica_groups=mesh['phi'=64,'row'=4] {'row'}, dimensions={1}, use_global_device_ids=true | all-gather | bytes 40960 | tf_op jit(solution)/shard_map/all_gather | solution.py:157
  334.4 1.6 stack.41
  336.0 9.4 %all-to-all-start = ((f32[64,16,512]{2,1,0:T(8,128)}), f32[64,16,512]{2,1,0:T(8,128)S(1)}, u32[]{:S(2)}, u32[]{:S(2)}) async-start(f32[64,16,512]{2,1,0:T(8,128)} %stack.41), calls=%async_computation | async-start | bytes 4194304 | tf_op jit(solution)/shard_map/all_to_all | solution.py:159
  347.7 49.0 %all-to-all-done = f32[64,16,512]{2,1,0:T(8,128)S(1)} async-done(((f32[64,16,512]{2,1,0:T(8,128)}), f32[64,16,512]{2,1,0:T(8,128)S(1)}, u32[]{:S(2)}, u32[]{:S(2)}) %all-to-all-start) | async-done | bytes 2097184 | tf_op jit(solution)/shard_map/all_to_all | solution.py:159
  398.0 2.1 copy.45
  400.1 23.0 %gather_fusion.3 = f32[4096]{0:T(1024)S(1)} fusion(f32[524288]{0:T(1024)S(1)} %bitcast.63, s32[4096]{0:T(1024)S(1)} %bitcast_clamp_fusion), kind=kCustom, calls=%fused_computation.3.clone | custom fusion | bytes 49152 | tf_op jit(solution)/shard_map/jit(_take)/gather | solution.py:111
  423.2 23.0 %gather_fusion.2 = f32[4096]{0:T(1024)S(1)} fusion(f32[524288]{0:T(1024)S(1)} %bitcast.64, s32[4096]{0:T(1024)S(1)} %bitcast_clamp_fusion.1), kind=kCustom, calls=%fused_computation.2.clone | custom fusion | bytes 49152 | tf_op jit(solution)/shard_map/jit(_take)/gather | solution.py:111
  446.2 23.0 %gather_fusion.1 = f32[4096]{0:T(1024)S(1)} fusion(f32[524288]{0:T(1024)S(1)} %bitcast.65, s32[4096]{0:T(1024)S(1)} %bitcast_clamp_fusion.2), kind=kCustom, calls=%fused_computation.1.clone | custom fusion | bytes 49152 | tf_op jit(solution)/shard_map/jit(_take)/gather | solution.py:111
  469.3 23.0 %gather_fusion = f32[4096]{0:T(1024)S(1)} fusion(f32[524288]{0:T(1024)S(1)} %bitcast.66, s32[4096]{0:T(1024)S(1)} %bitcast_clamp_fusion.3), kind=kCustom, calls=%fused_computation.clone | custom fusion | bytes 49152 | tf_op jit(solution)/shard_map/jit(_take)/gather | solution.py:111
  (187 shorter events, 35.3 us)
Async XLA Ops:
  4.1 9.4 %collective-permute-start.3 = (f32[4,16,32,1]{2,1,3,0:T(8,128)S(1)}, f32[4,16,32,1]{2,1,3,0:T(8,128)S(1)}, u32[]{:S(2)}, u32[]{:S(2)}) collective-permute-start(f32[4,16,32,1]{2,1,3,0:T(8,128)S(1)} %copy.36), channel_id=1, source_target_pairs={{1,0},{2,1},{3,2},{5,4},{6,5},{7,6},{9,8},{10,9},{11,10},{13,12},{... | collective-permute-start | bytes 24584 | tf_op jit(solution)/shard_map/ppermute | solution.py:25
  6.5 7.6 %collective-permute-start.2 = (f32[4,16,32,1]{2,1,3,0:T(8,128)}, f32[4,16,32,1]{2,1,3,0:T(8,128)}, u32[]{:S(2)}, u32[]{:S(2)}) collective-permute-start(f32[4,16,32,1]{2,1,3,0:T(8,128)} %copy.35), channel_id=1, source_target_pairs={{0,1},{1,2},{2,3},{4,5},{5,6},{6,7},{8,9},{9,10},{10,11},{12,13},{... | collective-permute-start | bytes 24584 | tf_op jit(solution)/shard_map/ppermute | solution.py:23
  10.9 9.8 %collective-permute-start.1 = (f32[4,1,32,128]{3,1,2,0:T(1,128)}, f32[4,1,32,128]{3,1,2,0:T(1,128)S(1)}, u32[]{:S(2)}, u32[]{:S(2)}) collective-permute-start(f32[4,1,32,128]{3,1,2,0:T(1,128)} %get-tuple-element.146), channel_id=1, source_target_pairs={{4,0},{8,4},{12,8},{16,12},{20,16},{24,20},{28,24},{32,28},{36,32}... | collective-permute-start | bytes 196616 | tf_op jit(solution)/shard_map/ppermute | solution.py:25
  12.4 8.2 %collective-permute-start = (f32[4,1,32,128]{3,1,2,0:T(1,128)}, f32[4,1,32,128]{3,1,2,0:T(1,128)}, u32[]{:S(2)}, u32[]{:S(2)}) collective-permute-start(f32[4,1,32,128]{3,1,2,0:T(1,128)} %get-tuple-element.145), channel_id=1, source_target_pairs={{0,4},{4,8},{8,12},{12,16},{16,20},{20,24},{24,28},{28,32},{32,36}... | collective-permute-start | bytes 196616 | tf_op jit(solution)/shard_map/ppermute | solution.py:23
  24.0 27.8 %collective-permute-start.4 = (f32[4,16,32,128]{3,1,2,0:T(8,128)S(1)}, f32[4,16,32,128]{3,1,2,0:T(8,128)S(1)}, u32[]{:S(2)}, u32[]{:S(2)}) collective-permute-start(f32[4,16,32,128]{3,1,2,0:T(8,128)S(1)} %pad_maximum_fusion.14), channel_id=1, source_target_pairs={{0,4},{4,8},{8,12},{12,16},{16,20},{20,24},{24,28},{28,32},{32,36}... | collective-permute-start | bytes 3145736 | tf_op jit(solution)/shard_map/ppermute | solution.py:35
  26.8 87.9 %copy-start.9 = (pred[128]{0:T(512)(128)(4,1)}, pred[128]{0:T(512)(128)(4,1)S(1)}, u32[]{:S(2)}) copy-start(pred[128]{0:T(512)(128)(4,1)S(1)} %get-tuple-element.175) | copy-start | bytes 388
  51.9 34.1 %collective-permute-start.5 = (f32[4,16,32,128]{3,1,2,0:T(8,128)S(1)}, f32[4,16,32,128]{3,1,2,0:T(8,128)S(1)}, u32[]{:S(2)}, u32[]{:S(2)}) collective-permute-start(f32[4,16,32,128]{3,1,2,0:T(8,128)S(1)} %broadcast_select_fusion.1), channel_id=1, source_target_pairs={{0,8},{4,12},{8,16},{12,20},{16,24},{20,28},{24,32},{28,36},{32,40... | collective-permute-start | bytes 3145736 | tf_op jit(solution)/shard_map/ppermute | solution.py:35
  86.2 28.5 %collective-permute-start.6 = (f32[4,16,32,128]{3,1,2,0:T(8,128)S(1)}, f32[4,16,32,128]{3,1,2,0:T(8,128)S(1)}, u32[]{:S(2)}, u32[]{:S(2)}) collective-permute-start(f32[4,16,32,128]{3,1,2,0:T(8,128)S(1)} %broadcast_select_fusion.3), channel_id=1, source_target_pairs={{0,16},{4,20},{8,24},{12,28},{16,32},{20,36},{24,40},{28,44},{32,4... | collective-permute-start | bytes 3145736 | tf_op jit(solution)/shard_map/ppermute | solution.py:35
  114.9 24.8 %collective-permute-start.7 = (f32[4,16,32,128]{3,1,2,0:T(8,128)S(1)}, f32[4,16,32,128]{3,1,2,0:T(8,128)S(1)}, u32[]{:S(2)}, u32[]{:S(2)}) collective-permute-start(f32[4,16,32,128]{3,1,2,0:T(8,128)S(1)} %broadcast_select_fusion.5), channel_id=1, source_target_pairs={{0,32},{4,36},{8,40},{12,44},{16,48},{20,52},{24,56},{28,60},{32,6... | collective-permute-start | bytes 3145736 | tf_op jit(solution)/shard_map/ppermute | solution.py:35
  139.8 23.6 %collective-permute-start.8 = (f32[4,16,32,128]{3,1,2,0:T(8,128)S(1)}, f32[4,16,32,128]{3,1,2,0:T(8,128)S(1)}, u32[]{:S(2)}, u32[]{:S(2)}) collective-permute-start(f32[4,16,32,128]{3,1,2,0:T(8,128)S(1)} %broadcast_select_fusion.7), channel_id=1, source_target_pairs={{0,4},{4,8},{8,12},{12,16},{16,20},{20,24},{24,28},{28,32},{32,36}... | collective-permute-start | bytes 3145736 | tf_op jit(solution)/shard_map/ppermute | solution.py:35
  169.7 11.9 %collective-permute-start.12 = (f32[4,16,32,1]{2,1,3,0:T(8,128)S(1)}, f32[4,16,32,1]{2,1,3,0:T(8,128)}, u32[]{:S(2)}, u32[]{:S(2)}) collective-permute-start(f32[4,16,32,1]{2,1,3,0:T(8,128)S(1)} %copy.40), channel_id=1, source_target_pairs={{1,0},{2,1},{3,2},{5,4},{6,5},{7,6},{9,8},{10,9},{11,10},{13,12},{... | collective-permute-start | bytes 24584 | tf_op jit(solution)/shard_map/ppermute | solution.py:25
  172.0 10.8 %collective-permute-start.11 = (f32[4,16,32,1]{2,1,3,0:T(8,128)}, f32[4,16,32,1]{2,1,3,0:T(8,128)}, u32[]{:S(2)}, u32[]{:S(2)}) collective-permute-start(f32[4,16,32,1]{2,1,3,0:T(8,128)} %copy.39), channel_id=1, source_target_pairs={{0,1},{1,2},{2,3},{4,5},{5,6},{6,7},{8,9},{9,10},{10,11},{12,13},{... | collective-permute-start | bytes 24584 | tf_op jit(solution)/shard_map/ppermute | solution.py:23
  177.2 12.2 %collective-permute-start.10 = (f32[4,1,32,128]{3,1,2,0:T(1,128)}, f32[4,1,32,128]{3,1,2,0:T(1,128)S(1)}, u32[]{:S(2)}, u32[]{:S(2)}) collective-permute-start(f32[4,1,32,128]{3,1,2,0:T(1,128)} %get-tuple-element.130), channel_id=1, source_target_pairs={{4,0},{8,4},{12,8},{16,12},{20,16},{24,20},{28,24},{32,28},{36,32}... | collective-permute-start | bytes 196616 | tf_op jit(solution)/shard_map/ppermute | solution.py:25
  181.4 8.7 %collective-permute-start.9 = (f32[4,1,32,128]{3,1,2,0:T(1,128)}, f32[4,1,32,128]{3,1,2,0:T(1,128)}, u32[]{:S(2)}, u32[]{:S(2)}) collective-permute-start(f32[4,1,32,128]{3,1,2,0:T(1,128)} %get-tuple-element.129), channel_id=1, source_target_pairs={{0,4},{4,8},{8,12},{12,16},{16,20},{20,24},{24,28},{28,32},{32,36}... | collective-permute-start | bytes 196616 | tf_op jit(solution)/shard_map/ppermute | solution.py:23
  193.4 27.9 %collective-permute-start.13 = (f32[4,16,32,128]{3,1,2,0:T(8,128)S(1)}, f32[4,16,32,128]{3,1,2,0:T(8,128)S(1)}, u32[]{:S(2)}, u32[]{:S(2)}) collective-permute-start(f32[4,16,32,128]{3,1,2,0:T(8,128)S(1)} %pad_maximum_fusion.15), channel_id=1, source_target_pairs={{0,4},{4,8},{8,12},{12,16},{16,20},{20,24},{24,28},{28,32},{32,36}... | collective-permute-start | bytes 3145736 | tf_op jit(solution)/shard_map/ppermute | solution.py:35
  221.4 55.4 %copy-start.10 = (pred[128]{0:T(512)(128)(4,1)S(1)}, pred[128]{0:T(512)(128)(4,1)}, u32[]{:S(2)}) copy-start(pred[128]{0:T(512)(128)(4,1)} %copy-done.9) | copy-start | bytes 388
  221.4 27.6 %collective-permute-start.14 = (f32[4,16,32,128]{3,1,2,0:T(8,128)S(1)}, f32[4,16,32,128]{3,1,2,0:T(8,128)S(1)}, u32[]{:S(2)}, u32[]{:S(2)}) collective-permute-start(f32[4,16,32,128]{3,1,2,0:T(8,128)S(1)} %broadcast_select_fusion), channel_id=1, source_target_pairs={{0,8},{4,12},{8,16},{12,20},{16,24},{20,28},{24,32},{28,36},{32,40... | collective-permute-start | bytes 3145736 | tf_op jit(solution)/shard_map/ppermute | solution.py:35
  249.3 27.5 %collective-permute-start.15 = (f32[4,16,32,128]{3,1,2,0:T(8,128)S(1)}, f32[4,16,32,128]{3,1,2,0:T(8,128)S(1)}, u32[]{:S(2)}, u32[]{:S(2)}) collective-permute-start(f32[4,16,32,128]{3,1,2,0:T(8,128)S(1)} %broadcast_select_fusion.2), channel_id=1, source_target_pairs={{0,16},{4,20},{8,24},{12,28},{16,32},{20,36},{24,40},{28,44},{32,4... | collective-permute-start | bytes 3145736 | tf_op jit(solution)/shard_map/ppermute | solution.py:35
  277.0 46.7 %copy-start.8 = (f32[128]{0:T(128)S(1)}, f32[128]{0:T(128)}, u32[]{:S(2)}) copy-start(f32[128]{0:T(128)} %copy-done.7) | copy-start | bytes 1540
  277.0 46.7 %copy-start.12 = (pred[128]{0:T(512)(128)(4,1)S(1)}, pred[128]{0:T(512)(128)(4,1)}, u32[]{:S(2)}) copy-start(pred[128]{0:T(512)(128)(4,1)} %copy-done.11) | copy-start | bytes 388
  277.0 46.7 %copy-start.14 = (pred[128]{0:T(512)(128)(4,1)S(1)}, pred[128]{0:T(512)(128)(4,1)}, u32[]{:S(2)}) copy-start(pred[128]{0:T(512)(128)(4,1)} %copy-done.13) | copy-start | bytes 388
  277.0 46.7 %copy-start.16 = (pred[128]{0:T(512)(128)(4,1)S(1)}, pred[128]{0:T(512)(128)(4,1)}, u32[]{:S(2)}) copy-start(pred[128]{0:T(512)(128)(4,1)} %copy-done.15) | copy-start | bytes 388
  277.0 46.7 %copy-start.18 = (pred[128]{0:T(512)(128)(4,1)S(1)}, pred[128]{0:T(512)(128)(4,1)}, u32[]{:S(2)}) copy-start(pred[128]{0:T(512)(128)(4,1)} %copy-done.17) | copy-start | bytes 388
  277.0 46.7 %copy-start.20 = (pred[128]{0:T(512)(128)(4,1)S(1)}, pred[128]{0:T(512)(128)(4,1)}, u32[]{:S(2)}) copy-start(pred[128]{0:T(512)(128)(4,1)} %copy-done.19) | copy-start | bytes 388
  277.0 46.7 %copy-start.22 = (pred[128]{0:T(512)(128)(4,1)S(1)}, pred[128]{0:T(512)(128)(4,1)}, u32[]{:S(2)}) copy-start(pred[128]{0:T(512)(128)(4,1)} %copy-done.21) | copy-start | bytes 388
  277.0 46.7 %copy-start.24 = (pred[128]{0:T(512)(128)(4,1)S(1)}, pred[128]{0:T(512)(128)(4,1)}, u32[]{:S(2)}) copy-start(pred[128]{0:T(512)(128)(4,1)} %copy-done.23) | copy-start | bytes 388
  277.0 46.7 %copy-start.26 = (pred[128]{0:T(512)(128)(4,1)S(1)}, pred[128]{0:T(512)(128)(4,1)}, u32[]{:S(2)}) copy-start(pred[128]{0:T(512)(128)(4,1)} %copy-done.25) | copy-start | bytes 388
  277.0 46.7 %copy-start.28 = (pred[128]{0:T(512)(128)(4,1)S(1)}, pred[128]{0:T(512)(128)(4,1)}, u32[]{:S(2)}) copy-start(pred[128]{0:T(512)(128)(4,1)} %copy-done.27) | copy-start | bytes 388
  277.1 46.7 %copy-start.30 = (pred[128]{0:T(512)(128)(4,1)S(1)}, pred[128]{0:T(512)(128)(4,1)}, u32[]{:S(2)}) copy-start(pred[128]{0:T(512)(128)(4,1)} %copy-done.29) | copy-start | bytes 388
  277.1 21.5 %collective-permute-start.16 = (f32[4,16,32,128]{3,1,2,0:T(8,128)S(1)}, f32[4,16,32,128]{3,1,2,0:T(8,128)S(1)}, u32[]{:S(2)}, u32[]{:S(2)}) collective-permute-start(f32[4,16,32,128]{3,1,2,0:T(8,128)S(1)} %broadcast_select_fusion.4), channel_id=1, source_target_pairs={{0,32},{4,36},{8,40},{12,44},{16,48},{20,52},{24,56},{28,60},{32,6... | collective-permute-start | bytes 3145736 | tf_op jit(solution)/shard_map/ppermute | solution.py:35
  298.8 24.9 %collective-permute-start.17 = (f32[4,16,32,128]{3,1,2,0:T(8,128)S(1)}, f32[4,16,32,128]{3,1,2,0:T(8,128)S(1)}, u32[]{:S(2)}, u32[]{:S(2)}) collective-permute-start(f32[4,16,32,128]{3,1,2,0:T(8,128)S(1)} %broadcast_select_fusion.6), channel_id=1, source_target_pairs={{0,4},{4,8},{8,12},{12,16},{16,20},{20,24},{24,28},{28,32},{32,36}... | collective-permute-start | bytes 3145736 | tf_op jit(solution)/shard_map/ppermute | solution.py:35
  336.0 60.7 %all-to-all-start = ((f32[64,16,512]{2,1,0:T(8,128)}), f32[64,16,512]{2,1,0:T(8,128)S(1)}, u32[]{:S(2)}, u32[]{:S(2)}) async-start(f32[64,16,512]{2,1,0:T(8,128)} %stack.41), calls=%async_computation | async-start | bytes 4194304 | tf_op jit(solution)/shard_map/all_to_all | solution.py:159
  (30 other events, 667.5 us)
